TPU v7x, 32 devices: a whole 2x2x4 slice. The times are simulated.
32 devices in a mesh: section: 4 (over z), space: 8 (over y, x, core).
Axes of the slice: x: 2, y: 2, z: 4, core: 2. Of those that a mesh axis runs over, the one named last changes fastest.
Arguments:
- features: bfloat16 [1, 32, 128, 320], P(None, 'space'), may hold values from -30 to 30
- section_packs: bfloat16 [4, 11520, 640], P('section', None, 'space'), may hold values from -6 to 6
Outputs:
- output: bfloat16 [1, 32, 128, 320], P(None, 'space', 'section')
All inputs are finite; a program needn't handle non-finite values.
Results may differ from a plain program's by a relative error of at most 0.009.
Values may be sent and summed in bfloat16 or wider, within the bound.
No kernel may reach another device: no remote copies, remote signals or barrier semaphores. Data moves between devices by JAX's collectives and lax.ppermute only.
A program may use at most 128 MiB of HBM per device.

v0:
```python
from functools import partial
import math
import jax
import jax.numpy as jnp
from jax import lax
from jax.sharding import PartitionSpec as P

GROUPS = 32
EPSILON = 1e-05


def for_sending(x):
    return jax.tree.map(lambda a: a.astype(jnp.bfloat16) if a.dtype == jnp.float32 else a, x)


def padded(x, sides, width):
    for axis, dim in sides:
        size, length = (lax.axis_size(axis), x.shape[dim])
        up = [(i, (i + 1) % size) for i in range(size - 1)]
        down = [(j, i) for i, j in up]
        last = lax.slice_in_dim(x, length - width, length, axis=dim)
        initial = lax.slice_in_dim(x, 0, width, axis=dim)
        before = lax.ppermute(last, axis, up)
        after = lax.ppermute(initial, axis, down)
        x = jnp.concatenate([before, x, after], axis=dim)
    return x


def passed_along(value, axis, steps):
    count = lax.axis_size(axis)
    initial, last = (max(0, -steps), min(count, count - steps))
    return lax.ppermute(value, axis, [(source, source + steps) for source in range(initial, last)])


def convolve_rows(field_ext, kernel, fan_in, stride):
    result = lax.conv_general_dilated(
        field_ext[None],
        kernel,
        (stride, stride),
        ((0, 0), (1, 1)),
        dimension_numbers=("NHWC", "HWIO", "NHWC"),
        preferred_element_type=jnp.float32,
    )[0]
    return result * (1.0 / math.sqrt(fan_in))


def kernel_at(flat_pack, offset, c_in, c_out):
    return flat_pack[offset : offset + 9 * c_in * c_out].reshape(3, 3, c_in, c_out)


def grouped_view(values):
    return values.reshape(-1, GROUPS, values.shape[-1] // GROUPS)


def normalize(values, group_mean, group_var):
    shape_in = values.shape
    grouped = values.reshape(shape_in[:-1] + (GROUPS, shape_in[-1] // GROUPS))
    normed = (grouped - group_mean[:, None]) / jnp.sqrt(group_var + EPSILON)[:, None]
    return normed.reshape(shape_in)


def activate_ext(raw_ext, group_mean, group_var, top_edge, bottom_edge, ghost_rows):
    activated = jax.nn.silu(normalize(raw_ext.astype(jnp.float32), group_mean, group_var))
    row_ids = lax.broadcasted_iota(jnp.int32, (raw_ext.shape[0], 1, 1), 0)
    dropped = (row_ids < ghost_rows) & top_edge | (
        row_ids >= raw_ext.shape[0] - ghost_rows
    ) & bottom_edge
    return jnp.where(dropped, 0.0, activated).astype(jnp.bfloat16)


def edge_rows(block, ghost_rows):
    return jnp.concatenate(
        [
            block[:ghost_rows].reshape(ghost_rows, -1),
            block[block.shape[0] - ghost_rows :].reshape(ghost_rows, -1),
        ],
        0,
    )


def add_rows(cycle_rows, block, ghost_rows):
    row_shape = (ghost_rows,) + block.shape[1:]
    return jnp.concatenate(
        [
            cycle_rows[:ghost_rows].reshape(row_shape),
            block,
            cycle_rows[3 * ghost_rows :].reshape(row_shape),
        ],
        0,
    )


def trim_rows(block, count):
    return block[count : block.shape[0] - count]


def branches(func):
    return [
        partial(func, 0),
        partial(func, 1),
        partial(func, 2),
        partial(func, 3),
        partial(func, 4),
    ]


def shards(features, section_packs):
    section_id = lax.axis_index("section")
    row_dev = lax.axis_index("space")
    n_space = lax.axis_size("space")
    top_edge = row_dev == 0
    bottom_edge = row_dev == n_space - 1
    micro_count, fine_rows, fine_cols, narrow = features.shape
    wide_ch = 2 * narrow
    square = narrow * narrow
    fine_shape = (fine_rows, fine_cols, narrow)
    coarse_shape = (fine_rows // 2, fine_cols // 2, wide_ch)
    fine_zero = jnp.zeros(fine_shape, jnp.bfloat16)
    coarse_zero = jnp.zeros(coarse_shape, jnp.bfloat16)
    is_fine = (section_id == 0) | (section_id == 3)
    gathered = lax.all_gather(section_packs, "space", axis=2, tiled=True)
    flat_pack = gathered.reshape(-1)
    ghost_rows = 1

    def row_rims(block_rims):
        return padded(for_sending(block_rims), (("space", 0),), 1).astype(block_rims.dtype)

    spare = ghost_rows - 1
    fine_hidden_zero = jnp.zeros((fine_rows + 2 * spare, fine_cols, narrow), jnp.bfloat16)
    coarse_hidden_zero = jnp.zeros(
        (fine_rows // 2 + 2 * spare, fine_cols // 2, wide_ch), jnp.bfloat16
    )

    def moments(branch_pick, source):
        empty = jnp.zeros((GROUPS,), jnp.float32)

        def pair_sums(branch_id):
            if branch_id == 4:
                return (empty, empty)
            grouped = grouped_view(source(branch_id))
            factor = 1.0 / (grouped.shape[0] * grouped.shape[2] * n_space)
            return (
                jnp.sum(grouped, axis=(0, 2)) * factor,
                jnp.sum(jnp.square(grouped), axis=(0, 2)) * factor,
            )

        first_part, second_part = lax.switch(branch_pick, branches(pair_sums))
        group_mean, mean_square = lax.psum((first_part, second_part), "space")
        return (group_mean, mean_square - group_mean * group_mean)

    def section_tick(tick_id, loop_state):
        handoff, skip_store, results = loop_state
        micro_id = tick_id - section_id
        active = (micro_id >= 0) & (micro_id < micro_count)
        micro_slot = jnp.clip(micro_id, 0, micro_count - 1)
        branch_pick = jnp.where(active, section_id, 4)
        skip_ext = lax.dynamic_index_in_dim(skip_store, micro_slot, 0, keepdims=False)
        skip_inner = trim_rows(skip_ext, ghost_rows)
        cycle_in = row_rims(edge_rows(handoff, ghost_rows))

        def section_entry(branch_id):
            if branch_id == 0:
                return (
                    lax.dynamic_index_in_dim(features, micro_slot, 0, keepdims=False),
                    coarse_zero,
                )
            if branch_id == 3:
                coarse_ext = trim_rows(add_rows(cycle_in, handoff, ghost_rows), spare)
                upsampled = jnp.repeat(jnp.repeat(coarse_ext, 2, 0), 2, 1)[1:-1]
                made = convolve_rows(
                    upsampled, kernel_at(flat_pack, 0, wide_ch, narrow), 9 * wide_ch, 1
                )
                return (made.astype(jnp.bfloat16), coarse_zero)
            if branch_id == 4:
                return (fine_zero, coarse_zero)
            return (fine_zero, handoff)

        fine_in, coarse_in = lax.switch(branch_pick, branches(section_entry))

        def block_input(branch_id):
            if branch_id == 0:
                return fine_in.astype(jnp.float32)
            if branch_id == 3:
                return jnp.concatenate([fine_in, skip_inner], -1).astype(jnp.float32)
            return coarse_in.astype(jnp.float32)

        mean_one, var_one = moments(branch_pick, block_input)
        cycle_one = row_rims(
            jnp.where(is_fine, edge_rows(fine_in, ghost_rows), edge_rows(coarse_in, ghost_rows))
        )

        def first_conv(branch_id):
            if branch_id == 4:
                return (fine_hidden_zero, coarse_hidden_zero)
            if branch_id in (1, 2):
                activated = activate_ext(
                    add_rows(cycle_one, coarse_in, ghost_rows),
                    mean_one,
                    var_one,
                    top_edge,
                    bottom_edge,
                    ghost_rows,
                )
                made = convolve_rows(
                    activated, kernel_at(flat_pack, 0, wide_ch, wide_ch), 9 * wide_ch, 1
                )
                return (fine_hidden_zero, made.astype(jnp.bfloat16))
            raw_ext = add_rows(cycle_one, fine_in, ghost_rows)
            c_in = narrow
            offset = 0
            if branch_id == 3:
                raw_ext = jnp.concatenate([raw_ext, skip_ext], -1)
                c_in = wide_ch
                offset = 18 * square
            activated = activate_ext(raw_ext, mean_one, var_one, top_edge, bottom_edge, ghost_rows)
            made = convolve_rows(activated, kernel_at(flat_pack, offset, c_in, narrow), 9 * c_in, 1)
            return (made.astype(jnp.bfloat16), coarse_hidden_zero)

        hidden_fine, hidden_coarse = lax.switch(branch_pick, branches(first_conv))

        def hidden_input(branch_id):
            if branch_id in (0, 3):
                return trim_rows(hidden_fine, spare).astype(jnp.float32)
            return trim_rows(hidden_coarse, spare).astype(jnp.float32)

        mean_two, var_two = moments(branch_pick, hidden_input)
        cycle_two = row_rims(
            jnp.where(is_fine, edge_rows(hidden_fine, 1), edge_rows(hidden_coarse, 1))
        )
        fine_hidden_ext = add_rows(cycle_two, hidden_fine, 1)
        coarse_hidden_ext = add_rows(cycle_two, hidden_coarse, 1)

        def second_conv(branch_id):
            if branch_id == 4:
                return (fine_zero, coarse_zero)
            if branch_id in (1, 2):
                activated = activate_ext(
                    coarse_hidden_ext, mean_two, var_two, top_edge, bottom_edge, 1
                )
                update = convolve_rows(
                    activated, kernel_at(flat_pack, 36 * square, wide_ch, wide_ch), 9 * wide_ch, 1
                )
                return (fine_zero, (coarse_in.astype(jnp.float32) + update).astype(jnp.bfloat16))
            activated = activate_ext(fine_hidden_ext, mean_two, var_two, top_edge, bottom_edge, 1)
            if branch_id == 0:
                update = convolve_rows(
                    activated, kernel_at(flat_pack, 9 * square, narrow, narrow), 9 * narrow, 1
                )
                return ((fine_in.astype(jnp.float32) + update).astype(jnp.bfloat16), coarse_zero)
            update = convolve_rows(
                activated, kernel_at(flat_pack, 36 * square, narrow, narrow), 9 * narrow, 1
            )
            joined = jnp.concatenate([fine_in, skip_inner], -1)
            projection = jnp.dot(
                joined.reshape(-1, wide_ch),
                flat_pack[45 * square : 47 * square].reshape(wide_ch, narrow),
                preferred_element_type=jnp.float32,
            )
            projection = projection.reshape(fine_shape) * (1.0 / math.sqrt(wide_ch))
            return ((projection + update).astype(jnp.bfloat16), coarse_zero)

        out_fine, out_coarse = lax.switch(branch_pick, branches(second_conv))
        cycle_three = row_rims(edge_rows(out_fine, ghost_rows))
        made_skip = add_rows(cycle_three, out_fine, ghost_rows)

        def section_exit(branch_id):
            if branch_id == 0:
                made = convolve_rows(
                    trim_rows(made_skip, spare),
                    kernel_at(flat_pack, 18 * square, narrow, wide_ch),
                    9 * narrow,
                    2,
                )
                return made.astype(jnp.bfloat16)
            if branch_id in (1, 2):
                return out_coarse
            return coarse_zero

        coarse_out = lax.switch(branch_pick, branches(section_exit))
        next_handoff = jax.tree.map(
            lambda part, own: part.astype(own.dtype),
            passed_along(for_sending(coarse_out), "section", 1),
            coarse_out,
        )
        incoming = passed_along(for_sending(made_skip), "section", 3).astype(made_skip.dtype)
        store_here = (section_id == 3) & (tick_id < micro_count)
        store_slot = jnp.clip(tick_id, 0, micro_count - 1)
        current = lax.dynamic_index_in_dim(skip_store, store_slot, 0, keepdims=False)
        skip_store = lax.dynamic_update_index_in_dim(
            skip_store, jnp.where(store_here, incoming, current), store_slot, 0
        )
        result_now = lax.dynamic_index_in_dim(results, micro_slot, 0, keepdims=False)
        results = lax.dynamic_update_index_in_dim(
            results, jnp.where((section_id == 3) & active, out_fine, result_now), micro_slot, 0
        )
        return (next_handoff, skip_store, results)

    skip_start = jnp.zeros(
        (micro_count, fine_rows + 2 * ghost_rows, fine_cols, narrow), jnp.bfloat16
    )
    result_start = jnp.zeros((micro_count,) + fine_shape, jnp.bfloat16)
    final_state = lax.fori_loop(
        0, micro_count + 3, section_tick, (coarse_zero, skip_start, result_start)
    )
    results = final_state[2]
    return lax.psum_scatter(
        results.astype(jnp.float32).astype(jnp.bfloat16), "section", scatter_dimension=2, tiled=True
    )


def solution(mesh):
    return jax.shard_map(
        shards,
        mesh=mesh,
        in_specs=(P(None, "space", None, None), P("section", None, "space")),
        out_specs=P(None, "space", "section", None),
        check_vma=False,
    )
```

profile of v0, /device:TPU:0, one launch (start us, length us, event | category | flops | bytes accessed | tf_op | source)
XLA Modules:
  0.0 817.5 jit_solution(6047263199579071338)
XLA Ops:
  7.3 85.8 %all-gather.2.cloned.1.call-done = bf16[1,11520,640]{1,2,0:T(8,128)(2,1)} async-done(((bf16[1,11520,80]{1,2,0:T(8,128)(2,1)}), bf16[1,11520,640]{1,2,0:T(8,128)(2,1)}) %all-gather.2.cloned.1.call-update) | async-done | bytes 14745616 | tf_op jit(solution)/shard_map/all_gather | solution.py:121
  93.1 18.7 %copy.218 = bf16[1,11520,640]{2,1,0:T(8,128)(2,1)} copy(bf16[1,11520,640]{1,2,0:T(8,128)(2,1)} %all-gather.2.cloned.1.call-done) | data formatting | bytes 29491200 | tf_op jit(solution)/shard_map/all_gather | solution.py:121
  111.8 24.4 %reshape.795 = bf16[7372800]{0:T(1024)(128)(2,1)} reshape(bf16[1,11520,640]{2,1,0:T(8,128)(2,1)} %copy.218) | data formatting | bytes 29491200 | tf_op jit(solution)/shard_map/reshape | solution.py:122
  137.2 641.9 %while.24 = (s32[]{:T(128)}, bf16[2,64,640]{2,0,1:T(2,128)(2,1)S(1)}, bf16[1,6,128,320]{2,3,1,0:T(8,128)(2,1)S(1)}, bf16[1,4,128,320]{2,3,1,0:T(8,128)(2,1)}, s3...) while((s32[]{:T(128)}, ...), condition=%wide.region_67.68_spmd, body=%wide.region_0.67_spmd.sunk | while | flops 5784842240 | bytes 176676080 | solution.py:302
  139.1 3.0 collective-permute-start
  143.1 4.8 conditional.12
  150.6 2.2 collective-permute-start.2
  154.7 15.0 %all-reduce.4 = (f32[32]{0:T(128)S(1)}, f32[32]{0:T(128)S(1)}) all-reduce(f32[32]{0:T(128)S(1)} %get-tuple-element.957, f32[32]{0:T(128)S(1)} %get-tuple-element.958), channel_id=1, replica_groups=mesh['section'=4,'space'=8] {'space'}, use_global_device_ids=true, to_apply=%region_27.27 | all-reduce | flops 64 | bytes 512 | tf_op jit(solution)/shard_map/while/body/eval_jaxpr/psum | solution.py:148
  169.7 27.9 %conditional.14 = (bf16[4,128,320]{2,0,1:T(4,128)(2,1)S(1)}, bf16[2,64,640]{2,1,0:T(8,128)(2,1)}, bf16[2,64,640]{2,0,1:T(2,128)(2,1)}, bf16[1,40960]{1,0:T(2,128)(2,1)S(1)}, bf16[1,40960]{1,0:T(2,128)(2,1)S(1)}) conditional(s32[]{:T(128)} %clamp.14, (pred[]{:T(512)}, pred[]{:T(512)}, bf16[1,40960]{1,0:T(2,128)(2,1)S(1)}, ...), branch_computations={%region_29.29_spmd.clone, %region_30.30_spmd.clone, %region_31.31_... | conditional | flops 2017290240 | bytes 48206080 | solution.py:219
  170.5 1.7 slice.311
  173.8 3.1 reshape.944
  178.2 3.4 fusion.129
  203.1 3.0 collective-permute-done.5
  207.5 17.3 %all-reduce.5 = (f32[32]{0:T(128)S(1)}, f32[32]{0:T(128)S(1)}) all-reduce(f32[32]{0:T(128)S(1)} %get-tuple-element.971, f32[32]{0:T(128)S(1)} %get-tuple-element.972), channel_id=1, replica_groups=mesh['section'=4,'space'=8] {'space'}, use_global_device_ids=true, to_apply=%region_55.55 | all-reduce | flops 64 | bytes 512 | tf_op jit(solution)/shard_map/while/body/eval_jaxpr/psum | solution.py:148
  224.9 2.2 pad_maximum_fusion.6
  227.1 19.0 %conditional.16 = (bf16[4,128,320]{1,2,0:T(8,128)(2,1)S(1)}, bf16[2,64,640]{2,1,0:T(8,128)(2,1)S(1)}) conditional(s32[]{:T(128)} %clamp.14, (bf16[4,128,320]{2,0,1:T(4,128)(2,1)S(1)}, pred[]{:T(512)}, pred[]{:T(512)}, bf16[6,128,320]{2,1,0:T(8,128)(2,1)S(1)}, f32[32]{0:T(128)S(1)}, /*index=5*/f32[32]{0:T(128)S(1)}, ...), branch_computations={%region_57.57_spmd, %region_58.58_spmd, %region_59.59_spmd, %regio... | conditional | flops 1218529280 | bytes 43285440 | solution.py:262
  230.1 3.1 reshape.774
  233.1 3.5 fusion.9
  250.1 2.8 collective-permute-done.6
  254.5 2.1 collective-permute-start.9
  257.4 16.4 %conditional.17 = (bf16[2,64,640]{2,0,1:T(2,128)(2,1)S(1)}) conditional(s32[]{:T(128)} %clamp.14, (bf16[6,128,320]{1,2,0:T(8,128)(2,1)}, bf16[7372800]{0:T(1024)(128)(2,1)}) %tuple.329, bf16[2,64,640]{2,1,0:T(8,128)(2,1)S(1)} %get-tuple-element.979, bf16[2,64,640]{2,1,0:T(8,128)(2,1)S(1)} %get-tuple-element.979, ...), branch_computations={%region_62.62_spmd, %region_63.63_spmd, %region_64.64_spmd, %regio... | conditional | flops 532961280 | bytes 24266638 | solution.py:279
  257.5 3.4 slice.261
  261.0 7.2 slice.262
  270.4 2.9 fusion.75
  275.2 2.7 collective-permute-done.8
  282.2 7.6 collective-permute-start
  293.9 6.7 collective-permute-start.2
  302.0 15.4 %all-reduce.4 = (f32[32]{0:T(128)S(1)}, f32[32]{0:T(128)S(1)}) all-reduce(f32[32]{0:T(128)S(1)} %get-tuple-element.957, f32[32]{0:T(128)S(1)} %get-tuple-element.958), channel_id=1, replica_groups=mesh['section'=4,'space'=8] {'space'}, use_global_device_ids=true, to_apply=%region_27.27 | all-reduce | flops 64 | bytes 512 | tf_op jit(solution)/shard_map/while/body/eval_jaxpr/psum | solution.py:148
  317.4 15.1 %conditional.14 = (bf16[4,128,320]{2,0,1:T(4,128)(2,1)S(1)}, bf16[2,64,640]{2,1,0:T(8,128)(2,1)}, bf16[2,64,640]{2,0,1:T(2,128)(2,1)}, bf16[1,40960]{1,0:T(2,128)(2,1)S(1)}, bf16[1,40960]{1,0:T(2,128)(2,1)S(1)}) conditional(s32[]{:T(128)} %clamp.14, (pred[]{:T(512)}, pred[]{:T(512)}, bf16[1,40960]{1,0:T(2,128)(2,1)S(1)}, ...), branch_computations={%region_29.29_spmd.clone, %region_30.30_spmd.clone, %region_31.31_... | conditional | flops 2017290240 | bytes 48206080 | solution.py:219
  334.8 1.8 collective-permute-start.4
  338.6 3.1 collective-permute-done.5
  342.6 17.7 %all-reduce.5 = (f32[32]{0:T(128)S(1)}, f32[32]{0:T(128)S(1)}) all-reduce(f32[32]{0:T(128)S(1)} %get-tuple-element.971, f32[32]{0:T(128)S(1)} %get-tuple-element.972), channel_id=1, replica_groups=mesh['section'=4,'space'=8] {'space'}, use_global_device_ids=true, to_apply=%region_55.55 | all-reduce | flops 64 | bytes 512 | tf_op jit(solution)/shard_map/while/body/eval_jaxpr/psum | solution.py:148
  360.3 2.2 pad_maximum_fusion.6
  362.5 8.7 %conditional.16 = (bf16[4,128,320]{1,2,0:T(8,128)(2,1)S(1)}, bf16[2,64,640]{2,1,0:T(8,128)(2,1)S(1)}) conditional(s32[]{:T(128)} %clamp.14, (bf16[4,128,320]{2,0,1:T(4,128)(2,1)S(1)}, pred[]{:T(512)}, pred[]{:T(512)}, bf16[6,128,320]{2,1,0:T(8,128)(2,1)S(1)}, f32[32]{0:T(128)S(1)}, /*index=5*/f32[32]{0:T(128)S(1)}, ...), branch_computations={%region_57.57_spmd, %region_58.58_spmd, %region_59.59_spmd, %regio... | conditional | flops 1218529280 | bytes 43285440 | solution.py:262
  375.2 2.8 collective-permute-done.6
  379.6 2.1 collective-permute-start.9
  384.0 47.7 %collective-permute-start.8 = (bf16[2,64,640]{2,0,1:T(2,128)(2,1)S(1)}, bf16[2,64,640]{2,0,1:T(2,128)(2,1)S(1)}, u32[]{:S(2)}, u32[]{:S(2)}) collective-permute-start(bf16[2,64,640]{2,0,1:T(2,128)(2,1)S(1)} %get-tuple-element.1090), channel_id=1, source_target_pairs={{0,8},{8,16},{16,24},{1,9},{9,17},{17,25},{2,10},{10,18},{18,26},{... | collective-permute-start | bytes 491528 | tf_op jit(solution)/shard_map/while/body/eval_jaxpr/ppermute | solution.py:32
  431.7 2.7 collective-permute-done.8
  436.2 6.8 collective-permute-start
  447.6 6.2 collective-permute-start.2
  455.1 15.6 %all-reduce.4 = (f32[32]{0:T(128)S(1)}, f32[32]{0:T(128)S(1)}) all-reduce(f32[32]{0:T(128)S(1)} %get-tuple-element.957, f32[32]{0:T(128)S(1)} %get-tuple-element.958), channel_id=1, replica_groups=mesh['section'=4,'space'=8] {'space'}, use_global_device_ids=true, to_apply=%region_27.27 | all-reduce | flops 64 | bytes 512 | tf_op jit(solution)/shard_map/while/body/eval_jaxpr/psum | solution.py:148
  470.8 15.1 %conditional.14 = (bf16[4,128,320]{2,0,1:T(4,128)(2,1)S(1)}, bf16[2,64,640]{2,1,0:T(8,128)(2,1)}, bf16[2,64,640]{2,0,1:T(2,128)(2,1)}, bf16[1,40960]{1,0:T(2,128)(2,1)S(1)}, bf16[1,40960]{1,0:T(2,128)(2,1)S(1)}) conditional(s32[]{:T(128)} %clamp.14, (pred[]{:T(512)}, pred[]{:T(512)}, bf16[1,40960]{1,0:T(2,128)(2,1)S(1)}, ...), branch_computations={%region_29.29_spmd.clone, %region_30.30_spmd.clone, %region_31.31_... | conditional | flops 2017290240 | bytes 48206080 | solution.py:219
  491.7 3.1 collective-permute-done.5
  495.7 17.7 %all-reduce.5 = (f32[32]{0:T(128)S(1)}, f32[32]{0:T(128)S(1)}) all-reduce(f32[32]{0:T(128)S(1)} %get-tuple-element.971, f32[32]{0:T(128)S(1)} %get-tuple-element.972), channel_id=1, replica_groups=mesh['section'=4,'space'=8] {'space'}, use_global_device_ids=true, to_apply=%region_55.55 | all-reduce | flops 64 | bytes 512 | tf_op jit(solution)/shard_map/while/body/eval_jaxpr/psum | solution.py:148
  513.4 2.2 pad_maximum_fusion.6
  515.6 8.7 %conditional.16 = (bf16[4,128,320]{1,2,0:T(8,128)(2,1)S(1)}, bf16[2,64,640]{2,1,0:T(8,128)(2,1)S(1)}) conditional(s32[]{:T(128)} %clamp.14, (bf16[4,128,320]{2,0,1:T(4,128)(2,1)S(1)}, pred[]{:T(512)}, pred[]{:T(512)}, bf16[6,128,320]{2,1,0:T(8,128)(2,1)S(1)}, f32[32]{0:T(128)S(1)}, /*index=5*/f32[32]{0:T(128)S(1)}, ...), branch_computations={%region_57.57_spmd, %region_58.58_spmd, %region_59.59_spmd, %regio... | conditional | flops 1218529280 | bytes 43285440 | solution.py:262
  528.3 2.8 collective-permute-done.6
  532.7 2.1 collective-permute-start.9
  537.1 4.1 collective-permute-start.8
  541.6 4.1 collective-permute-done.8
  547.5 6.2 collective-permute-start
  558.9 5.6 collective-permute-start.2
  565.9 17.2 %all-reduce.4 = (f32[32]{0:T(128)S(1)}, f32[32]{0:T(128)S(1)}) all-reduce(f32[32]{0:T(128)S(1)} %get-tuple-element.957, f32[32]{0:T(128)S(1)} %get-tuple-element.958), channel_id=1, replica_groups=mesh['section'=4,'space'=8] {'space'}, use_global_device_ids=true, to_apply=%region_27.27 | all-reduce | flops 64 | bytes 512 | tf_op jit(solution)/shard_map/while/body/eval_jaxpr/psum | solution.py:148
  583.1 15.1 %conditional.14 = (bf16[4,128,320]{2,0,1:T(4,128)(2,1)S(1)}, bf16[2,64,640]{2,1,0:T(8,128)(2,1)}, bf16[2,64,640]{2,0,1:T(2,128)(2,1)}, bf16[1,40960]{1,0:T(2,128)(2,1)S(1)}, bf16[1,40960]{1,0:T(2,128)(2,1)S(1)}) conditional(s32[]{:T(128)} %clamp.14, (pred[]{:T(512)}, pred[]{:T(512)}, bf16[1,40960]{1,0:T(2,128)(2,1)S(1)}, ...), branch_computations={%region_29.29_spmd.clone, %region_30.30_spmd.clone, %region_31.31_... | conditional | flops 2017290240 | bytes 48206080 | solution.py:219
  603.8 3.0 collective-permute-done.5
  607.6 17.7 %all-reduce.5 = (f32[32]{0:T(128)S(1)}, f32[32]{0:T(128)S(1)}) all-reduce(f32[32]{0:T(128)S(1)} %get-tuple-element.971, f32[32]{0:T(128)S(1)} %get-tuple-element.972), channel_id=1, replica_groups=mesh['section'=4,'space'=8] {'space'}, use_global_device_ids=true, to_apply=%region_55.55 | all-reduce | flops 64 | bytes 512 | tf_op jit(solution)/shard_map/while/body/eval_jaxpr/psum | solution.py:148
  625.3 2.2 pad_maximum_fusion.6
  627.6 8.7 %conditional.16 = (bf16[4,128,320]{1,2,0:T(8,128)(2,1)S(1)}, bf16[2,64,640]{2,1,0:T(8,128)(2,1)S(1)}) conditional(s32[]{:T(128)} %clamp.14, (bf16[4,128,320]{2,0,1:T(4,128)(2,1)S(1)}, pred[]{:T(512)}, pred[]{:T(512)}, bf16[6,128,320]{2,1,0:T(8,128)(2,1)S(1)}, f32[32]{0:T(128)S(1)}, /*index=5*/f32[32]{0:T(128)S(1)}, ...), branch_computations={%region_57.57_spmd, %region_58.58_spmd, %region_59.59_spmd, %regio... | conditional | flops 1218529280 | bytes 43285440 | solution.py:262
  640.2 2.8 collective-permute-done.6
  644.6 122.9 %collective-permute-start.9 = (bf16[6,128,320]{1,2,0:T(8,128)(2,1)}, bf16[6,128,320]{1,2,0:T(8,128)(2,1)}, u32[]{:S(2)}, u32[]{:S(2)}) collective-permute-start(bf16[6,128,320]{1,2,0:T(8,128)(2,1)} %pad_maximum_fusion.7), channel_id=1, source_target_pairs={{0,24},{1,25},{2,26},{3,27},{4,28},{5,29},{6,30},{7,31}} | collective-permute-start | bytes 1474568 | tf_op jit(solution)/shard_map/while/body/eval_jaxpr/ppermute | solution.py:32
  771.1 3.4 collective-permute-done.9
  774.6 3.3 collective-permute-done.8
  779.2 1.9 copy.219
  781.1 29.3 %reduce-scatter.2.cloned.1.call-done = bf16[1,4,32,320]{3,2,1,0:T(8,128)(2,1)} async-done(((bf16[1,4,128,320]{3,2,1,0:T(8,128)(2,1)}), bf16[1,4,32,320]{3,2,1,0:T(8,128)(2,1)}) %reduce-scatter.2.cloned.1.call-update) | async-done | bytes 81936 | tf_op jit(solution)/shard_map/reduce_scatter | solution.py:306
  (376 shorter events, 108.5 us)
Async XLA Ops:
  6.5 86.6 %all-gather.2.cloned.1.call-start = ((), (), s32[]{:S(2)}) async-start(), calls=%async_computation.1 | async-start | bytes 16588800 | tf_op jit(solution)/shard_map/all_gather | solution.py:121
  7.3 803.1 %reduce-scatter.2.cloned.1.call-start = ((), (), s32[]{:S(2)}) async-start(), calls=%async_computation.2 | async-start | bytes 491520 | tf_op jit(solution)/shard_map/reduce_scatter | solution.py:306
  137.8 4.7 collective-permute-start.1
  139.1 4.0 collective-permute-start
  142.5 11.5 %copy-start = (bf16[4,128,320]{2,1,0:T(8,128)(2,1)}, bf16[4,128,320]{2,1,0:T(8,128)(2,1)S(1)}, u32[]{:S(2)}) copy-start(bf16[4,128,320]{2,1,0:T(8,128)(2,1)S(1)} %slice_bitcast_fusion.19) | copy-start | bytes 983044 | tf_op jit(solution)/shard_map/while
  150.6 19.1 %collective-permute-start.2 = (bf16[1,40960]{1,0:T(2,128)(2,1)S(1)}, bf16[1,40960]{1,0:T(2,128)(2,1)S(1)}, u32[]{:S(2)}, u32[]{:S(2)}) collective-permute-start(bf16[1,40960]{1,0:T(2,128)(2,1)S(1)} %get-tuple-element.955), channel_id=1, source_target_pairs={{0,1},{1,2},{2,3},{3,4},{4,5},{5,6},{6,7},{8,9},{9,10},{10,11},{11... | collective-permute-start | bytes 245768 | tf_op jit(solution)/shard_map/while/body/eval_jaxpr/ppermute | solution.py:23
  152.7 17.0 %collective-permute-start.3 = (bf16[1,40960]{1,0:T(2,128)(2,1)S(1)}, bf16[1,40960]{1,0:T(2,128)(2,1)S(1)}, u32[]{:S(2)}, u32[]{:S(2)}) collective-permute-start(bf16[1,40960]{1,0:T(2,128)(2,1)S(1)} %get-tuple-element.956), channel_id=1, source_target_pairs={{1,0},{2,1},{3,2},{4,3},{5,4},{6,5},{7,6},{9,8},{10,9},{11,10},{12... | collective-permute-start | bytes 245768 | tf_op jit(solution)/shard_map/while/body/eval_jaxpr/ppermute | solution.py:24
  169.7 0.7 copy-start.6
  170.5 2.1 copy-start.7
  170.5 2.6 copy-start.5
  177.5 0.7 copy-start.13
  199.9 2.6 collective-permute-start.4
  201.2 4.9 collective-permute-start.5
  206.7 20.4 %copy-start.1 = (bf16[4,128,320]{2,1,0:T(8,128)(2,1)S(1)}, bf16[4,128,320]{2,1,0:T(8,128)(2,1)}, u32[]{:S(2)}) copy-start(bf16[4,128,320]{2,1,0:T(8,128)(2,1)} %copy-done) | copy-start | bytes 983044 | tf_op jit(solution)/shard_map/while
  230.0 3.1 copy-start.16
  246.1 10.5 %copy-start.10 = (bf16[1,4,128,320]{2,3,1,0:T(8,128)(2,1)S(1)}, bf16[1,4,128,320]{2,3,1,0:T(8,128)(2,1)}, u32[]{:S(2)}) copy-start(bf16[1,4,128,320]{2,3,1,0:T(8,128)(2,1)} %get-tuple-element.1063) | copy-start | bytes 983044 | tf_op jit(solution)/shard_map/while
  246.4 2.9 collective-permute-start.7
  248.0 4.9 collective-permute-start.6
  254.5 20.6 %collective-permute-start.9 = (bf16[6,128,320]{1,2,0:T(8,128)(2,1)}, bf16[6,128,320]{1,2,0:T(8,128)(2,1)}, u32[]{:S(2)}, u32[]{:S(2)}) collective-permute-start(bf16[6,128,320]{1,2,0:T(8,128)(2,1)} %pad_maximum_fusion.7), channel_id=1, source_target_pairs={{0,24},{1,25},{2,26},{3,27},{4,28},{5,29},{6,30},{7,31}} | collective-permute-start | bytes 1474568 | tf_op jit(solution)/shard_map/while/body/eval_jaxpr/ppermute | solution.py:32
  256.6 0.7 copy-start.11
  269.7 0.7 copy-start.21
  273.8 4.1 collective-permute-start.8
  280.9 9.3 %collective-permute-start.1 = (bf16[1,40960]{1,0:T(2,128)(2,1)S(1)}, bf16[1,40960]{1,0:T(2,128)(2,1)S(1)}, u32[]{:S(2)}, u32[]{:S(2)}) collective-permute-start(bf16[1,40960]{1,0:T(2,128)(2,1)S(1)} %bitcast.271), channel_id=1, source_target_pairs={{1,0},{2,1},{3,2},{4,3},{5,4},{6,5},{7,6},{9,8},{10,9},{11,10},{12... | collective-permute-start | bytes 245768 | tf_op jit(solution)/shard_map/while/body/eval_jaxpr/ppermute | solution.py:24
  282.2 8.7 %collective-permute-start = (bf16[1,40960]{1,0:T(2,128)(2,1)S(1)}, bf16[1,40960]{1,0:T(2,128)(2,1)S(1)}, u32[]{:S(2)}, u32[]{:S(2)}) collective-permute-start(bf16[1,40960]{1,0:T(2,128)(2,1)S(1)} %bitcast.270), channel_id=1, source_target_pairs={{0,1},{1,2},{2,3},{3,4},{4,5},{5,6},{6,7},{8,9},{9,10},{10,11},{11... | collective-permute-start | bytes 245768 | tf_op jit(solution)/shard_map/while/body/eval_jaxpr/ppermute | solution.py:23
  290.3 11.7 %copy-start = (bf16[4,128,320]{2,1,0:T(8,128)(2,1)}, bf16[4,128,320]{2,1,0:T(8,128)(2,1)S(1)}, u32[]{:S(2)}) copy-start(bf16[4,128,320]{2,1,0:T(8,128)(2,1)S(1)} %slice_bitcast_fusion.19) | copy-start | bytes 983044 | tf_op jit(solution)/shard_map/while
  293.9 23.5 %collective-permute-start.2 = (bf16[1,40960]{1,0:T(2,128)(2,1)S(1)}, bf16[1,40960]{1,0:T(2,128)(2,1)S(1)}, u32[]{:S(2)}, u32[]{:S(2)}) collective-permute-start(bf16[1,40960]{1,0:T(2,128)(2,1)S(1)} %get-tuple-element.955), channel_id=1, source_target_pairs={{0,1},{1,2},{2,3},{3,4},{4,5},{5,6},{6,7},{8,9},{9,10},{10,11},{11... | collective-permute-start | bytes 245768 | tf_op jit(solution)/shard_map/while/body/eval_jaxpr/ppermute | solution.py:23
  300.6 16.8 %collective-permute-start.3 = (bf16[1,40960]{1,0:T(2,128)(2,1)S(1)}, bf16[1,40960]{1,0:T(2,128)(2,1)S(1)}, u32[]{:S(2)}, u32[]{:S(2)}) collective-permute-start(bf16[1,40960]{1,0:T(2,128)(2,1)S(1)} %get-tuple-element.956), channel_id=1, source_target_pairs={{1,0},{2,1},{3,2},{4,3},{5,4},{6,5},{7,6},{9,8},{10,9},{11,10},{12... | collective-permute-start | bytes 245768 | tf_op jit(solution)/shard_map/while/body/eval_jaxpr/ppermute | solution.py:24
  334.8 3.1 collective-permute-start.4
  336.7 5.1 collective-permute-start.5
  342.3 20.2 %copy-start.1 = (bf16[4,128,320]{2,1,0:T(8,128)(2,1)S(1)}, bf16[4,128,320]{2,1,0:T(8,128)(2,1)}, u32[]{:S(2)}) copy-start(bf16[4,128,320]{2,1,0:T(8,128)(2,1)} %copy-done) | copy-start | bytes 983044 | tf_op jit(solution)/shard_map/while
  371.2 10.5 %copy-start.10 = (bf16[1,4,128,320]{2,3,1,0:T(8,128)(2,1)S(1)}, bf16[1,4,128,320]{2,3,1,0:T(8,128)(2,1)}, u32[]{:S(2)}) copy-start(bf16[1,4,128,320]{2,3,1,0:T(8,128)(2,1)} %get-tuple-element.1063) | copy-start | bytes 983044 | tf_op jit(solution)/shard_map/while
  371.5 2.9 collective-permute-start.7
  373.1 4.9 collective-permute-start.6
  379.6 52.0 %collective-permute-start.9 = (bf16[6,128,320]{1,2,0:T(8,128)(2,1)}, bf16[6,128,320]{1,2,0:T(8,128)(2,1)}, u32[]{:S(2)}, u32[]{:S(2)}) collective-permute-start(bf16[6,128,320]{1,2,0:T(8,128)(2,1)} %pad_maximum_fusion.7), channel_id=1, source_target_pairs={{0,24},{1,25},{2,26},{3,27},{4,28},{5,29},{6,30},{7,31}} | collective-permute-start | bytes 1474568 | tf_op jit(solution)/shard_map/while/body/eval_jaxpr/ppermute | solution.py:32
  381.7 0.7 copy-start.11
  384.0 50.5 %collective-permute-start.8 = (bf16[2,64,640]{2,0,1:T(2,128)(2,1)S(1)}, bf16[2,64,640]{2,0,1:T(2,128)(2,1)S(1)}, u32[]{:S(2)}, u32[]{:S(2)}) collective-permute-start(bf16[2,64,640]{2,0,1:T(2,128)(2,1)S(1)} %get-tuple-element.1090), channel_id=1, source_target_pairs={{0,8},{8,16},{16,24},{1,9},{9,17},{17,25},{2,10},{10,18},{18,26},{... | collective-permute-start | bytes 491528 | tf_op jit(solution)/shard_map/while/body/eval_jaxpr/ppermute | solution.py:32
  434.9 8.5 %collective-permute-start.1 = (bf16[1,40960]{1,0:T(2,128)(2,1)S(1)}, bf16[1,40960]{1,0:T(2,128)(2,1)S(1)}, u32[]{:S(2)}, u32[]{:S(2)}) collective-permute-start(bf16[1,40960]{1,0:T(2,128)(2,1)S(1)} %bitcast.271), channel_id=1, source_target_pairs={{1,0},{2,1},{3,2},{4,3},{5,4},{6,5},{7,6},{9,8},{10,9},{11,10},{12... | collective-permute-start | bytes 245768 | tf_op jit(solution)/shard_map/while/body/eval_jaxpr/ppermute | solution.py:24
  436.2 7.8 collective-permute-start
  443.4 11.7 %copy-start = (bf16[4,128,320]{2,1,0:T(8,128)(2,1)}, bf16[4,128,320]{2,1,0:T(8,128)(2,1)S(1)}, u32[]{:S(2)}) copy-start(bf16[4,128,320]{2,1,0:T(8,128)(2,1)S(1)} %slice_bitcast_fusion.19) | copy-start | bytes 983044 | tf_op jit(solution)/shard_map/while
  447.6 23.2 %collective-permute-start.2 = (bf16[1,40960]{1,0:T(2,128)(2,1)S(1)}, bf16[1,40960]{1,0:T(2,128)(2,1)S(1)}, u32[]{:S(2)}, u32[]{:S(2)}) collective-permute-start(bf16[1,40960]{1,0:T(2,128)(2,1)S(1)} %get-tuple-element.955), channel_id=1, source_target_pairs={{0,1},{1,2},{2,3},{3,4},{4,5},{5,6},{6,7},{8,9},{9,10},{10,11},{11... | collective-permute-start | bytes 245768 | tf_op jit(solution)/shard_map/while/body/eval_jaxpr/ppermute | solution.py:23
  453.7 17.0 %collective-permute-start.3 = (bf16[1,40960]{1,0:T(2,128)(2,1)S(1)}, bf16[1,40960]{1,0:T(2,128)(2,1)S(1)}, u32[]{:S(2)}, u32[]{:S(2)}) collective-permute-start(bf16[1,40960]{1,0:T(2,128)(2,1)S(1)} %get-tuple-element.956), channel_id=1, source_target_pairs={{1,0},{2,1},{3,2},{4,3},{5,4},{6,5},{7,6},{9,8},{10,9},{11,10},{12... | collective-permute-start | bytes 245768 | tf_op jit(solution)/shard_map/while/body/eval_jaxpr/ppermute | solution.py:24
  488.2 2.9 collective-permute-start.4
  489.8 5.1 collective-permute-start.5
  495.4 20.2 %copy-start.1 = (bf16[4,128,320]{2,1,0:T(8,128)(2,1)S(1)}, bf16[4,128,320]{2,1,0:T(8,128)(2,1)}, u32[]{:S(2)}) copy-start(bf16[4,128,320]{2,1,0:T(8,128)(2,1)} %copy-done) | copy-start | bytes 983044 | tf_op jit(solution)/shard_map/while
  524.3 10.5 %copy-start.10 = (bf16[1,4,128,320]{2,3,1,0:T(8,128)(2,1)S(1)}, bf16[1,4,128,320]{2,3,1,0:T(8,128)(2,1)}, u32[]{:S(2)}) copy-start(bf16[1,4,128,320]{2,3,1,0:T(8,128)(2,1)} %get-tuple-element.1063) | copy-start | bytes 983044 | tf_op jit(solution)/shard_map/while
  524.7 2.9 collective-permute-start.7
  526.3 4.9 collective-permute-start.6
  532.7 8.8 %collective-permute-start.9 = (bf16[6,128,320]{1,2,0:T(8,128)(2,1)}, bf16[6,128,320]{1,2,0:T(8,128)(2,1)}, u32[]{:S(2)}, u32[]{:S(2)}) collective-permute-start(bf16[6,128,320]{1,2,0:T(8,128)(2,1)} %pad_maximum_fusion.7), channel_id=1, source_target_pairs={{0,24},{1,25},{2,26},{3,27},{4,28},{5,29},{6,30},{7,31}} | collective-permute-start | bytes 1474568 | tf_op jit(solution)/shard_map/while/body/eval_jaxpr/ppermute | solution.py:32
  534.9 0.7 copy-start.11
  537.1 8.7 %collective-permute-start.8 = (bf16[2,64,640]{2,0,1:T(2,128)(2,1)S(1)}, bf16[2,64,640]{2,0,1:T(2,128)(2,1)S(1)}, u32[]{:S(2)}, u32[]{:S(2)}) collective-permute-start(bf16[2,64,640]{2,0,1:T(2,128)(2,1)S(1)} %get-tuple-element.1090), channel_id=1, source_target_pairs={{0,8},{8,16},{16,24},{1,9},{9,17},{17,25},{2,10},{10,18},{18,26},{... | collective-permute-start | bytes 491528 | tf_op jit(solution)/shard_map/while/body/eval_jaxpr/ppermute | solution.py:32
  546.2 7.9 collective-permute-start.1
  547.5 7.3 collective-permute-start
  554.1 11.7 %copy-start = (bf16[4,128,320]{2,1,0:T(8,128)(2,1)}, bf16[4,128,320]{2,1,0:T(8,128)(2,1)S(1)}, u32[]{:S(2)}) copy-start(bf16[4,128,320]{2,1,0:T(8,128)(2,1)S(1)} %slice_bitcast_fusion.19) | copy-start | bytes 983044 | tf_op jit(solution)/shard_map/while
  558.9 24.2 %collective-permute-start.2 = (bf16[1,40960]{1,0:T(2,128)(2,1)S(1)}, bf16[1,40960]{1,0:T(2,128)(2,1)S(1)}, u32[]{:S(2)}, u32[]{:S(2)}) collective-permute-start(bf16[1,40960]{1,0:T(2,128)(2,1)S(1)} %get-tuple-element.955), channel_id=1, source_target_pairs={{0,1},{1,2},{2,3},{3,4},{4,5},{5,6},{6,7},{8,9},{9,10},{10,11},{11... | collective-permute-start | bytes 245768 | tf_op jit(solution)/shard_map/while/body/eval_jaxpr/ppermute | solution.py:23
  564.5 18.6 %collective-permute-start.3 = (bf16[1,40960]{1,0:T(2,128)(2,1)S(1)}, bf16[1,40960]{1,0:T(2,128)(2,1)S(1)}, u32[]{:S(2)}, u32[]{:S(2)}) collective-permute-start(bf16[1,40960]{1,0:T(2,128)(2,1)S(1)} %get-tuple-element.956), channel_id=1, source_target_pairs={{1,0},{2,1},{3,2},{4,3},{5,4},{6,5},{7,6},{9,8},{10,9},{11,10},{12... | collective-permute-start | bytes 245768 | tf_op jit(solution)/shard_map/while/body/eval_jaxpr/ppermute | solution.py:24
  600.5 2.6 collective-permute-start.4
  601.8 4.9 collective-permute-start.5
  607.4 20.2 %copy-start.1 = (bf16[4,128,320]{2,1,0:T(8,128)(2,1)S(1)}, bf16[4,128,320]{2,1,0:T(8,128)(2,1)}, u32[]{:S(2)}) copy-start(bf16[4,128,320]{2,1,0:T(8,128)(2,1)} %copy-done) | copy-start | bytes 983044 | tf_op jit(solution)/shard_map/while
  636.2 131.3 %copy-start.10 = (bf16[1,4,128,320]{2,3,1,0:T(8,128)(2,1)S(1)}, bf16[1,4,128,320]{2,3,1,0:T(8,128)(2,1)}, u32[]{:S(2)}) copy-start(bf16[1,4,128,320]{2,3,1,0:T(8,128)(2,1)} %get-tuple-element.1063) | copy-start | bytes 983044 | tf_op jit(solution)/shard_map/while
  636.6 2.9 collective-permute-start.7
  638.2 4.9 collective-permute-start.6
  644.6 129.9 %collective-permute-start.9 = (bf16[6,128,320]{1,2,0:T(8,128)(2,1)}, bf16[6,128,320]{1,2,0:T(8,128)(2,1)}, u32[]{:S(2)}, u32[]{:S(2)}) collective-permute-start(bf16[6,128,320]{1,2,0:T(8,128)(2,1)} %pad_maximum_fusion.7), channel_id=1, source_target_pairs={{0,24},{1,25},{2,26},{3,27},{4,28},{5,29},{6,30},{7,31}} | collective-permute-start | bytes 1474568 | tf_op jit(solution)/shard_map/while/body/eval_jaxpr/ppermute | solution.py:32
  767.6 0.7 copy-start.11
  769.8 8.1 collective-permute-start.8
  (1 other events, 0.7 us)
Sparse Core Ops, SparseCore 0:
  9.2 83.8 all-gather.1
  781.2 29.1 reduce-scatter.1
where the time goes:
time: 823 us; the launch traced here: 818 us
  starting transfers between devices  260 us (32%)
  waiting for transfers between devices  158 us (19%)
  blocking collectives  134 us (16%)
  local copies, waits for them, and re-layouts  106 us (13%)
  loops' own time  106 us (13%)
  other arithmetic  29.3 us (4%)
  between operations  13.7 us (2%)
  matrix products  9.8 us (1%)
    ppermute x8, starting transfers between devices, passed_along(): lax.ppermute(value, axis, [(source, source + steps) for source in range(i...  183 us
    psum x8, blocking collectives, moments(): group_mean, mean_square = lax.psum((first_part, second_part), 'space')  134 us
    all_gather x1, waiting for transfers between devices, shards(): gathered = lax.all_gather(section_packs, 'space', axis=2, tiled=True)  85.8 us
    ppermute x16, starting transfers between devices, padded(): before = lax.ppermute(last, axis, up)  55.5 us
    another operation x4, loops' own time, section_tick(): hidden_fine, hidden_coarse = lax.switch(branch_pick, branches(first_conv))  54.2 us
    another operation x4, loops' own time, section_tick(): out_fine, out_coarse = lax.switch(branch_pick, branches(second_conv))  34.7 us
    reduce_scatter x1, waiting for transfers between devices, shards(): lax.psum_scatter(results.astype(jnp.float32).astype(jnp.bfloat16), 'secti...  29.3 us
    reshape x1, local copies, waits for them, and re-layouts, shards(): flat_pack = gathered.reshape(-1)  24.4 us
  transfers between devices with their start and end apart: 42, of which 20 were waited for; matrix products, arithmetic and copies ran while one was open for 3% of the time, Pallas kernels for 0%

commit v1 on v0

--- a/solution.py
+++ b/solution.py
@@ -118,7 +118,22 @@
     fine_zero = jnp.zeros(fine_shape, jnp.bfloat16)
     coarse_zero = jnp.zeros(coarse_shape, jnp.bfloat16)
     is_fine = (section_id == 0) | (section_id == 3)
-    gathered = lax.all_gather(section_packs, "space", axis=2, tiled=True)
+    g_now = lax.axis_size("space")
+    view_out = lax.axis_index("space")
+    e_next, newest, state_next = (g_now, view_out, section_packs.shape[2])
+    rack = []
+    for src_i in [*range(e_next)]:
+        rack.append((src_i, (src_i + 1) % e_next))
+    gathered = jnp.zeros(
+        (*section_packs.shape[:2], e_next * state_next, *section_packs.shape[3:]),
+        section_packs.dtype,
+    )
+    extra = section_packs
+    for k0 in [*range(e_next)]:
+        z2 = (newest - k0) % e_next
+        gathered = lax.dynamic_update_slice_in_dim(gathered, extra, z2 * state_next, axis=2)
+        if k0 < e_next - 1:
+            extra = lax.ppermute(extra, "space", rack)
     flat_pack = gathered.reshape(-1)
     ghost_rows = 1
 

time: 823 us -> 1140 us (1.39); the launches traced: 818 us -> 1120 us
  local copies, waits for them, and re-layouts: 106 us -> 377 us
  waiting for transfers between devices: 158 us -> 219 us
    dynamic_update_slice x0 -> x8, local copies, waits for them, and re-layouts: none -> 246 us  [shards(): lax.dynamic_update_slice_in_dim(gathered, extra, z2 * state_next, axis=2)]
    ppermute x0 -> x7, waiting for transfers between devices: none -> 142 us  [shards(): extra = lax.ppermute(extra, 'space', rack)]
    all_gather x1 -> x0, waiting for transfers between devices: 85.8 us -> none  [shards(): gathered = lax.all_gather(section_packs, 'space', axis=2, tiled=True)]
    ppermute x0 -> x7, local copies, waits for them, and re-layouts: none -> 27.6 us  [shards(): extra = lax.ppermute(extra, 'space', rack)]
    all_gather x1 -> x0, local copies, waits for them, and re-layouts: 18.7 us -> none  [shards(): gathered = lax.all_gather(section_packs, 'space', axis=2, tiled=True)]
  transfers between devices with their start and end apart: 42 -> 48, of which waited for: 20 -> 25; matrix products, arithmetic and copies ran while one was open for 3% -> 24% of each run, Pallas kernels for 0% -> 0%
where the time goes in v1:
time: 1140 us; the launch traced here: 1120 us
  local copies, waits for them, and re-layouts  377 us (33%)
  starting transfers between devices  249 us (22%)
  waiting for transfers between devices  219 us (19%)
  blocking collectives  126 us (11%)
  loops' own time  102 us (9%)
  other arithmetic  26.2 us (2%)
  between operations  13.9 us (1%)
    dynamic_update_slice x8, local copies, waits for them, and re-layouts, shards(): lax.dynamic_update_slice_in_dim(gathered, extra, z2 * state_next, axis=2)  246 us
    ppermute x8, starting transfers between devices, passed_along(): lax.ppermute(value, axis, [(source, source + steps) for source in range(i...  174 us
    ppermute x7, waiting for transfers between devices, shards(): extra = lax.ppermute(extra, 'space', rack)  142 us
    psum x8, blocking collectives, moments(): group_mean, mean_square = lax.psum((first_part, second_part), 'space')  126 us
    ppermute x16, starting transfers between devices, padded(): before = lax.ppermute(last, axis, up)  53.4 us
    another operation x4, loops' own time, section_tick(): hidden_fine, hidden_coarse = lax.switch(branch_pick, branches(first_conv))  51.3 us
    another operation x4, loops' own time, section_tick(): out_fine, out_coarse = lax.switch(branch_pick, branches(second_conv))  34.2 us
    ppermute x7, local copies, waits for them, and re-layouts, shards(): extra = lax.ppermute(extra, 'space', rack)  27.6 us
  transfers between devices with their start and end apart: 48, of which 25 were waited for; matrix products, arithmetic and copies ran while one was open for 24% of the time, Pallas kernels for 0%

profile of v1, /device:TPU:0, one launch (start us, length us, event | category | flops | bytes accessed | tf_op | source)
XLA Modules:
  0.0 1122.9 jit_solution(11714566228729851973)
XLA Ops:
  7.0 24.1 %collective-permute-done.10 = bf16[1,11520,80]{1,2,0:T(8,128)(2,1)S(1)} collective-permute-done((bf16[1,11520,80]{1,2,0:T(8,128)(2,1)}, bf16[1,11520,80]{1,2,0:T(8,128)(2,1)S(1)}, u32[]{:S(2)}, u32[]{:S(2)}) %collective-permute-start.10) | collective-permute-done | bytes 1843232 | tf_op jit(solution)/shard_map/ppermute | solution.py:136
  32.4 23.6 %collective-permute-done.11 = bf16[1,11520,80]{1,2,0:T(8,128)(2,1)S(1)} collective-permute-done((bf16[1,11520,80]{1,2,0:T(8,128)(2,1)S(1)}, bf16[1,11520,80]{1,2,0:T(8,128)(2,1)S(1)}, u32[]{:S(2)}, u32[]{:S(2)}) %collective-permute-start.11) | collective-permute-done | bytes 1843232 | tf_op jit(solution)/shard_map/ppermute | solution.py:136
  57.2 23.6 %collective-permute-done.12 = bf16[1,11520,80]{1,2,0:T(8,128)(2,1)S(1)} collective-permute-done((bf16[1,11520,80]{1,2,0:T(8,128)(2,1)S(1)}, bf16[1,11520,80]{1,2,0:T(8,128)(2,1)S(1)}, u32[]{:S(2)}, u32[]{:S(2)}) %collective-permute-start.12) | collective-permute-done | bytes 1843232 | tf_op jit(solution)/shard_map/ppermute | solution.py:136
  82.2 23.6 %collective-permute-done.13 = bf16[1,11520,80]{1,2,0:T(8,128)(2,1)S(1)} collective-permute-done((bf16[1,11520,80]{1,2,0:T(8,128)(2,1)S(1)}, bf16[1,11520,80]{1,2,0:T(8,128)(2,1)S(1)}, u32[]{:S(2)}, u32[]{:S(2)}) %collective-permute-start.13) | collective-permute-done | bytes 1843232 | tf_op jit(solution)/shard_map/ppermute | solution.py:136
  107.1 23.6 %collective-permute-done.14 = bf16[1,11520,80]{1,2,0:T(8,128)(2,1)S(1)} collective-permute-done((bf16[1,11520,80]{1,2,0:T(8,128)(2,1)S(1)}, bf16[1,11520,80]{1,2,0:T(8,128)(2,1)S(1)}, u32[]{:S(2)}, u32[]{:S(2)}) %collective-permute-start.14) | collective-permute-done | bytes 1843232 | tf_op jit(solution)/shard_map/ppermute | solution.py:136
  132.0 23.7 %collective-permute-done.15 = bf16[1,11520,80]{1,2,0:T(8,128)(2,1)} collective-permute-done((bf16[1,11520,80]{1,2,0:T(8,128)(2,1)S(1)}, bf16[1,11520,80]{1,2,0:T(8,128)(2,1)}, u32[]{:S(2)}, u32[]{:S(2)}) %collective-permute-start.15) | collective-permute-done | bytes 1843232 | tf_op jit(solution)/shard_map/ppermute | solution.py:136
  155.7 3.9 copy.232
  159.8 5.4 broadcast_in_dim.149
  165.2 27.3 %dynamic_update_slice.32 = bf16[1,11520,640]{2,1,0:T(8,128)(2,1)} dynamic-update-slice(bf16[1,11520,640]{2,1,0:T(8,128)(2,1)} %broadcast_in_dim.149, bf16[1,11520,80]{2,1,0:T(8,128)(2,1)S(1)} %copy.232, s32[]{:T(128)} %constant.302.clone.1, s32[]{:T(128)} %constant.302.clone.1, s32[]{:T(128)S(6)} %select_n.202) | dynamic-update-slice | bytes 3686404 | tf_op jit(solution)/shard_map/dynamic_update_slice | solution.py:134
  192.5 3.9 copy.233
  196.4 30.5 %dynamic_update_slice.33 = bf16[1,11520,640]{2,1,0:T(8,128)(2,1)} dynamic-update-slice(bf16[1,11520,640]{2,1,0:T(8,128)(2,1)} %dynamic_update_slice.32, bf16[1,11520,80]{2,1,0:T(8,128)(2,1)S(1)} %copy.233, s32[]{:T(128)} %constant.302.clone.1, s32[]{:T(128)} %constant.302.clone.1, s32[]{:T(128)S(6)} %select_n.204) | dynamic-update-slice | bytes 3686404 | tf_op jit(solution)/shard_map/dynamic_update_slice | solution.py:134
  226.9 3.9 copy.234
  230.8 31.4 %dynamic_update_slice.34 = bf16[1,11520,640]{2,1,0:T(8,128)(2,1)} dynamic-update-slice(bf16[1,11520,640]{2,1,0:T(8,128)(2,1)} %dynamic_update_slice.33, bf16[1,11520,80]{2,1,0:T(8,128)(2,1)S(1)} %copy.234, s32[]{:T(128)} %constant.302.clone.1, s32[]{:T(128)} %constant.302.clone.1, s32[]{:T(128)S(6)} %select_n.206) | dynamic-update-slice | bytes 3686404 | tf_op jit(solution)/shard_map/dynamic_update_slice | solution.py:134
  262.3 3.9 copy.235
  266.2 31.4 %dynamic_update_slice.35 = bf16[1,11520,640]{2,1,0:T(8,128)(2,1)} dynamic-update-slice(bf16[1,11520,640]{2,1,0:T(8,128)(2,1)} %dynamic_update_slice.34, bf16[1,11520,80]{2,1,0:T(8,128)(2,1)S(1)} %copy.235, s32[]{:T(128)} %constant.302.clone.1, s32[]{:T(128)} %constant.302.clone.1, s32[]{:T(128)S(6)} %select_n.208) | dynamic-update-slice | bytes 3686404 | tf_op jit(solution)/shard_map/dynamic_update_slice | solution.py:134
  297.7 3.9 copy.236
  301.6 31.4 %dynamic_update_slice.36 = bf16[1,11520,640]{2,1,0:T(8,128)(2,1)} dynamic-update-slice(bf16[1,11520,640]{2,1,0:T(8,128)(2,1)} %dynamic_update_slice.35, bf16[1,11520,80]{2,1,0:T(8,128)(2,1)S(1)} %copy.236, s32[]{:T(128)} %constant.302.clone.1, s32[]{:T(128)} %constant.302.clone.1, s32[]{:T(128)S(6)} %select_n.210) | dynamic-update-slice | bytes 3686404 | tf_op jit(solution)/shard_map/dynamic_update_slice | solution.py:134
  333.0 3.9 copy.237
  337.0 31.4 %dynamic_update_slice.37 = bf16[1,11520,640]{2,1,0:T(8,128)(2,1)} dynamic-update-slice(bf16[1,11520,640]{2,1,0:T(8,128)(2,1)} %dynamic_update_slice.36, bf16[1,11520,80]{2,1,0:T(8,128)(2,1)S(1)} %copy.237, s32[]{:T(128)} %constant.302.clone.1, s32[]{:T(128)} %constant.302.clone.1, s32[]{:T(128)S(6)} %select_n.212) | dynamic-update-slice | bytes 3686404 | tf_op jit(solution)/shard_map/dynamic_update_slice | solution.py:134
  368.4 3.9 copy.238
  372.4 31.4 %dynamic_update_slice.38 = bf16[1,11520,640]{2,1,0:T(8,128)(2,1)} dynamic-update-slice(bf16[1,11520,640]{2,1,0:T(8,128)(2,1)} %dynamic_update_slice.37, bf16[1,11520,80]{2,1,0:T(8,128)(2,1)S(1)} %copy.238, s32[]{:T(128)} %constant.302.clone.1, s32[]{:T(128)} %constant.302.clone.1, s32[]{:T(128)S(6)} %select_n.214) | dynamic-update-slice | bytes 3686404 | tf_op jit(solution)/shard_map/dynamic_update_slice | solution.py:134
  403.8 3.9 copy.239
  407.7 31.4 %dynamic_update_slice.39 = bf16[1,11520,640]{2,1,0:T(8,128)(2,1)} dynamic-update-slice(bf16[1,11520,640]{2,1,0:T(8,128)(2,1)} %dynamic_update_slice.38, bf16[1,11520,80]{2,1,0:T(8,128)(2,1)S(1)} %copy.239, s32[]{:T(128)} %constant.302.clone.1, s32[]{:T(128)} %constant.302.clone.1, s32[]{:T(128)S(6)} %select_n.216) | dynamic-update-slice | bytes 3686404 | tf_op jit(solution)/shard_map/dynamic_update_slice | solution.py:134
  439.2 24.4 %reshape.795 = bf16[7372800]{0:T(1024)(128)(2,1)} reshape(bf16[1,11520,640]{2,1,0:T(8,128)(2,1)} %dynamic_update_slice.39) | data formatting | bytes 29491200 | tf_op jit(solution)/shard_map/reshape | solution.py:137
  464.6 623.3 %while.24 = (s32[]{:T(128)}, bf16[2,64,640]{2,0,1:T(2,128)(2,1)S(1)}, bf16[1,6,128,320]{2,3,1,0:T(8,128)(2,1)S(1)}, bf16[1,4,128,320]{2,3,1,0:T(8,128)(2,1)}, s3...) while((s32[]{:T(128)}, ...), condition=%wide.region_67.68_spmd, body=%wide.region_0.67_spmd.sunk | while | flops 5784842240 | bytes 182410480 | solution.py:317
  470.5 4.7 conditional.12
  477.9 4.2 collective-permute-start.2
  484.0 13.2 %all-reduce.4 = (f32[32]{0:T(128)S(1)}, f32[32]{0:T(128)S(1)}) all-reduce(f32[32]{0:T(128)S(1)} %get-tuple-element.957, f32[32]{0:T(128)S(1)} %get-tuple-element.958), channel_id=1, replica_groups=mesh['section'=4,'space'=8] {'space'}, use_global_device_ids=true, to_apply=%region_27.27 | all-reduce | flops 64 | bytes 512 | tf_op jit(solution)/shard_map/while/body/eval_jaxpr/psum | solution.py:163
  497.3 26.9 %conditional.14 = (bf16[4,128,320]{2,0,1:T(4,128)(2,1)S(1)}, bf16[2,64,640]{2,1,0:T(8,128)(2,1)}, bf16[2,64,640]{2,0,1:T(2,128)(2,1)}, bf16[1,40960]{1,0:T(2,128)(2,1)S(1)}, bf16[1,40960]{1,0:T(2,128)(2,1)S(1)}) conditional(s32[]{:T(128)} %clamp.14, (pred[]{:T(512)}, pred[]{:T(512)}, bf16[1,40960]{1,0:T(2,128)(2,1)S(1)}, ...), branch_computations={%region_29.29_spmd.clone, %region_30.30_spmd.clone, %region_31.31_... | conditional | flops 2017290240 | bytes 56561976 | solution.py:234
  505.4 3.7 fusion.129
  533.3 17.7 %all-reduce.5 = (f32[32]{0:T(128)S(1)}, f32[32]{0:T(128)S(1)}) all-reduce(f32[32]{0:T(128)S(1)} %get-tuple-element.971, f32[32]{0:T(128)S(1)} %get-tuple-element.972), channel_id=1, replica_groups=mesh['section'=4,'space'=8] {'space'}, use_global_device_ids=true, to_apply=%region_55.55 | all-reduce | flops 64 | bytes 512 | tf_op jit(solution)/shard_map/while/body/eval_jaxpr/psum | solution.py:163
  552.5 18.8 %conditional.16 = (bf16[4,128,320]{1,2,0:T(8,128)(2,1)S(1)}, bf16[2,64,640]{2,1,0:T(8,128)(2,1)S(1)}) conditional(s32[]{:T(128)} %clamp.14, (bf16[4,128,320]{2,0,1:T(4,128)(2,1)S(1)}, pred[]{:T(512)}, pred[]{:T(512)}, bf16[6,128,320]{2,1,0:T(8,128)(2,1)S(1)}, f32[32]{0:T(128)S(1)}, /*index=5*/f32[32]{0:T(128)S(1)}, ...), branch_computations={%region_57.57_spmd, %region_58.58_spmd, %region_59.59_spmd, %regio... | conditional | flops 1218529280 | bytes 41974688 | solution.py:277
  558.6 3.5 fusion.9
  581.0 16.5 %conditional.17 = (bf16[2,64,640]{2,0,1:T(2,128)(2,1)S(1)}) conditional(s32[]{:T(128)} %clamp.14, (bf16[6,128,320]{1,2,0:T(8,128)(2,1)}, bf16[7372800]{0:T(1024)(128)(2,1)}) %tuple.329, bf16[2,64,640]{2,1,0:T(8,128)(2,1)S(1)} %get-tuple-element.979, bf16[2,64,640]{2,1,0:T(8,128)(2,1)S(1)} %get-tuple-element.979, ...), branch_computations={%region_62.62_spmd, %region_63.63_spmd, %region_64.64_spmd, %regio... | conditional | flops 532961280 | bytes 24266638 | solution.py:294
  583.2 3.4 slice.261
  586.6 7.2 slice.262
  604.6 4.1 collective-permute-start
  610.5 3.6 collective-permute-done.1
  617.2 6.6 collective-permute-start.2
  625.2 14.8 %all-reduce.4 = (f32[32]{0:T(128)S(1)}, f32[32]{0:T(128)S(1)}) all-reduce(f32[32]{0:T(128)S(1)} %get-tuple-element.957, f32[32]{0:T(128)S(1)} %get-tuple-element.958), channel_id=1, replica_groups=mesh['section'=4,'space'=8] {'space'}, use_global_device_ids=true, to_apply=%region_27.27 | all-reduce | flops 64 | bytes 512 | tf_op jit(solution)/shard_map/while/body/eval_jaxpr/psum | solution.py:163
  640.0 14.4 %conditional.14 = (bf16[4,128,320]{2,0,1:T(4,128)(2,1)S(1)}, bf16[2,64,640]{2,1,0:T(8,128)(2,1)}, bf16[2,64,640]{2,0,1:T(2,128)(2,1)}, bf16[1,40960]{1,0:T(2,128)(2,1)S(1)}, bf16[1,40960]{1,0:T(2,128)(2,1)S(1)}) conditional(s32[]{:T(128)} %clamp.14, (pred[]{:T(512)}, pred[]{:T(512)}, bf16[1,40960]{1,0:T(2,128)(2,1)S(1)}, ...), branch_computations={%region_29.29_spmd.clone, %region_30.30_spmd.clone, %region_31.31_... | conditional | flops 2017290240 | bytes 56561976 | solution.py:234
  663.7 17.7 %all-reduce.5 = (f32[32]{0:T(128)S(1)}, f32[32]{0:T(128)S(1)}) all-reduce(f32[32]{0:T(128)S(1)} %get-tuple-element.971, f32[32]{0:T(128)S(1)} %get-tuple-element.972), channel_id=1, replica_groups=mesh['section'=4,'space'=8] {'space'}, use_global_device_ids=true, to_apply=%region_55.55 | all-reduce | flops 64 | bytes 512 | tf_op jit(solution)/shard_map/while/body/eval_jaxpr/psum | solution.py:163
  682.9 8.7 conditional.16
  702.8 49.0 %collective-permute-start.8 = (bf16[2,64,640]{2,0,1:T(2,128)(2,1)S(1)}, bf16[2,64,640]{2,0,1:T(2,128)(2,1)S(1)}, u32[]{:S(2)}, u32[]{:S(2)}) collective-permute-start(bf16[2,64,640]{2,0,1:T(2,128)(2,1)S(1)} %get-tuple-element.1090), channel_id=1, source_target_pairs={{0,8},{8,16},{16,24},{1,9},{9,17},{17,25},{2,10},{10,18},{18,26},{... | collective-permute-start | bytes 491528 | tf_op jit(solution)/shard_map/while/body/eval_jaxpr/ppermute | solution.py:32
  760.6 5.0 collective-permute-done.1
  768.8 7.1 collective-permute-start.2
  777.3 13.4 %all-reduce.4 = (f32[32]{0:T(128)S(1)}, f32[32]{0:T(128)S(1)}) all-reduce(f32[32]{0:T(128)S(1)} %get-tuple-element.957, f32[32]{0:T(128)S(1)} %get-tuple-element.958), channel_id=1, replica_groups=mesh['section'=4,'space'=8] {'space'}, use_global_device_ids=true, to_apply=%region_27.27 | all-reduce | flops 64 | bytes 512 | tf_op jit(solution)/shard_map/while/body/eval_jaxpr/psum | solution.py:163
  790.7 14.3 %conditional.14 = (bf16[4,128,320]{2,0,1:T(4,128)(2,1)S(1)}, bf16[2,64,640]{2,1,0:T(8,128)(2,1)}, bf16[2,64,640]{2,0,1:T(2,128)(2,1)}, bf16[1,40960]{1,0:T(2,128)(2,1)S(1)}, bf16[1,40960]{1,0:T(2,128)(2,1)S(1)}) conditional(s32[]{:T(128)} %clamp.14, (pred[]{:T(512)}, pred[]{:T(512)}, bf16[1,40960]{1,0:T(2,128)(2,1)S(1)}, ...), branch_computations={%region_29.29_spmd.clone, %region_30.30_spmd.clone, %region_31.31_... | conditional | flops 2017290240 | bytes 56561976 | solution.py:234
  814.3 17.7 %all-reduce.5 = (f32[32]{0:T(128)S(1)}, f32[32]{0:T(128)S(1)}) all-reduce(f32[32]{0:T(128)S(1)} %get-tuple-element.971, f32[32]{0:T(128)S(1)} %get-tuple-element.972), channel_id=1, replica_groups=mesh['section'=4,'space'=8] {'space'}, use_global_device_ids=true, to_apply=%region_55.55 | all-reduce | flops 64 | bytes 512 | tf_op jit(solution)/shard_map/while/body/eval_jaxpr/psum | solution.py:163
  833.5 8.7 conditional.16
  853.4 3.7 collective-permute-start.8
  857.1 4.2 collective-permute-done.9
  861.4 3.3 collective-permute-done.8
  865.4 3.6 collective-permute-start
  870.7 4.7 collective-permute-done.1
  878.3 5.8 collective-permute-start.2
  885.5 13.5 %all-reduce.4 = (f32[32]{0:T(128)S(1)}, f32[32]{0:T(128)S(1)}) all-reduce(f32[32]{0:T(128)S(1)} %get-tuple-element.957, f32[32]{0:T(128)S(1)} %get-tuple-element.958), channel_id=1, replica_groups=mesh['section'=4,'space'=8] {'space'}, use_global_device_ids=true, to_apply=%region_27.27 | all-reduce | flops 64 | bytes 512 | tf_op jit(solution)/shard_map/while/body/eval_jaxpr/psum | solution.py:163
  898.9 14.4 %conditional.14 = (bf16[4,128,320]{2,0,1:T(4,128)(2,1)S(1)}, bf16[2,64,640]{2,1,0:T(8,128)(2,1)}, bf16[2,64,640]{2,0,1:T(2,128)(2,1)}, bf16[1,40960]{1,0:T(2,128)(2,1)S(1)}, bf16[1,40960]{1,0:T(2,128)(2,1)S(1)}) conditional(s32[]{:T(128)} %clamp.14, (pred[]{:T(512)}, pred[]{:T(512)}, bf16[1,40960]{1,0:T(2,128)(2,1)S(1)}, ...), branch_computations={%region_29.29_spmd.clone, %region_30.30_spmd.clone, %region_31.31_... | conditional | flops 2017290240 | bytes 56561976 | solution.py:234
  922.4 17.7 %all-reduce.5 = (f32[32]{0:T(128)S(1)}, f32[32]{0:T(128)S(1)}) all-reduce(f32[32]{0:T(128)S(1)} %get-tuple-element.971, f32[32]{0:T(128)S(1)} %get-tuple-element.972), channel_id=1, replica_groups=mesh['section'=4,'space'=8] {'space'}, use_global_device_ids=true, to_apply=%region_55.55 | all-reduce | flops 64 | bytes 512 | tf_op jit(solution)/shard_map/while/body/eval_jaxpr/psum | solution.py:163
  941.6 8.4 conditional.16
  957.6 115.0 %collective-permute-start.9 = (bf16[6,128,320]{1,2,0:T(8,128)(2,1)}, bf16[6,128,320]{1,2,0:T(8,128)(2,1)S(1)}, u32[]{:S(2)}, u32[]{:S(2)}) collective-permute-start(bf16[6,128,320]{1,2,0:T(8,128)(2,1)} %pad_maximum_fusion.7), channel_id=1, source_target_pairs={{0,24},{1,25},{2,26},{3,27},{4,28},{5,29},{6,30},{7,31}} | collective-permute-start | bytes 1474568 | tf_op jit(solution)/shard_map/while/body/eval_jaxpr/ppermute | solution.py:32
  1076.6 6.7 collective-permute-done.9
  1083.4 3.3 collective-permute-done.8
  1089.7 26.1 %reduce-scatter.2.cloned.1.call-done = bf16[1,4,32,320]{3,2,1,0:T(8,128)(2,1)} async-done(((bf16[1,4,128,320]{3,2,1,0:T(8,128)(2,1)}), bf16[1,4,32,320]{3,2,1,0:T(8,128)(2,1)}) %reduce-scatter.2.cloned.1.call-update) | async-done | bytes 81936 | tf_op jit(solution)/shard_map/reduce_scatter | solution.py:321
  (399 shorter events, 165.0 us)
Async XLA Ops:
  6.5 1109.3 %reduce-scatter.2.cloned.1.call-start = ((), (), s32[]{:S(2)}) async-start(), calls=%async_computation.1 | async-start | bytes 491520 | tf_op jit(solution)/shard_map/reduce_scatter | solution.py:321
  6.5 24.6 %collective-permute-start.10 = (bf16[1,11520,80]{1,2,0:T(8,128)(2,1)}, bf16[1,11520,80]{1,2,0:T(8,128)(2,1)S(1)}, u32[]{:S(2)}, u32[]{:S(2)}) collective-permute-start(bf16[1,11520,80]{1,2,0:T(8,128)(2,1)} %param.35), channel_id=1, source_target_pairs={{0,1},{1,2},{2,3},{3,4},{4,5},{5,6},{6,7},{7,0},{8,9},{9,10},{10,1... | collective-permute-start | bytes 5529608 | tf_op jit(solution)/shard_map/ppermute | solution.py:136
  31.1 1.2 copy-start.10
  32.4 23.6 %collective-permute-start.11 = (bf16[1,11520,80]{1,2,0:T(8,128)(2,1)S(1)}, bf16[1,11520,80]{1,2,0:T(8,128)(2,1)S(1)}, u32[]{:S(2)}, u32[]{:S(2)}) collective-permute-start(bf16[1,11520,80]{1,2,0:T(8,128)(2,1)S(1)} %collective-permute-done.10), channel_id=1, source_target_pairs={{0,1},{1,2},{2,3},{3,4},{4,5},{5,6},{6,7},{7,0},{8,9},{9,10},{10,1... | collective-permute-start | bytes 5529608 | tf_op jit(solution)/shard_map/ppermute | solution.py:136
  56.0 1.2 copy-start.11
  57.2 23.6 %collective-permute-start.12 = (bf16[1,11520,80]{1,2,0:T(8,128)(2,1)S(1)}, bf16[1,11520,80]{1,2,0:T(8,128)(2,1)S(1)}, u32[]{:S(2)}, u32[]{:S(2)}) collective-permute-start(bf16[1,11520,80]{1,2,0:T(8,128)(2,1)S(1)} %collective-permute-done.11), channel_id=1, source_target_pairs={{0,1},{1,2},{2,3},{3,4},{4,5},{5,6},{6,7},{7,0},{8,9},{9,10},{10,1... | collective-permute-start | bytes 5529608 | tf_op jit(solution)/shard_map/ppermute | solution.py:136
  80.9 1.3 copy-start.12
  82.2 23.6 %collective-permute-start.13 = (bf16[1,11520,80]{1,2,0:T(8,128)(2,1)S(1)}, bf16[1,11520,80]{1,2,0:T(8,128)(2,1)S(1)}, u32[]{:S(2)}, u32[]{:S(2)}) collective-permute-start(bf16[1,11520,80]{1,2,0:T(8,128)(2,1)S(1)} %collective-permute-done.12), channel_id=1, source_target_pairs={{0,1},{1,2},{2,3},{3,4},{4,5},{5,6},{6,7},{7,0},{8,9},{9,10},{10,1... | collective-permute-start | bytes 5529608 | tf_op jit(solution)/shard_map/ppermute | solution.py:136
  105.8 1.3 copy-start.13
  107.1 23.6 %collective-permute-start.14 = (bf16[1,11520,80]{1,2,0:T(8,128)(2,1)S(1)}, bf16[1,11520,80]{1,2,0:T(8,128)(2,1)S(1)}, u32[]{:S(2)}, u32[]{:S(2)}) collective-permute-start(bf16[1,11520,80]{1,2,0:T(8,128)(2,1)S(1)} %collective-permute-done.13), channel_id=1, source_target_pairs={{0,1},{1,2},{2,3},{3,4},{4,5},{5,6},{6,7},{7,0},{8,9},{9,10},{10,1... | collective-permute-start | bytes 5529608 | tf_op jit(solution)/shard_map/ppermute | solution.py:136
  130.7 1.2 copy-start.14
  132.0 23.7 %collective-permute-start.15 = (bf16[1,11520,80]{1,2,0:T(8,128)(2,1)S(1)}, bf16[1,11520,80]{1,2,0:T(8,128)(2,1)}, u32[]{:S(2)}, u32[]{:S(2)}) collective-permute-start(bf16[1,11520,80]{1,2,0:T(8,128)(2,1)S(1)} %collective-permute-done.14), channel_id=1, source_target_pairs={{0,1},{1,2},{2,3},{3,4},{4,5},{5,6},{6,7},{7,0},{8,9},{9,10},{10,1... | collective-permute-start | bytes 5529608 | tf_op jit(solution)/shard_map/ppermute | solution.py:136
  155.7 248.1 %collective-permute-start.16 = (bf16[1,11520,80]{1,2,0:T(8,128)(2,1)}, bf16[1,11520,80]{1,2,0:T(8,128)(2,1)}, u32[]{:S(2)}, u32[]{:S(2)}) collective-permute-start(bf16[1,11520,80]{1,2,0:T(8,128)(2,1)} %collective-permute-done.15), channel_id=1, source_target_pairs={{0,1},{1,2},{2,3},{3,4},{4,5},{5,6},{6,7},{7,0},{8,9},{9,10},{10,1... | collective-permute-start | bytes 5529608 | tf_op jit(solution)/shard_map/ppermute | solution.py:136
  465.3 3.0 collective-permute-start
  466.6 3.9 collective-permute-start.1
  468.3 15.1 %copy-start = (bf16[4,128,320]{2,1,0:T(8,128)(2,1)}, bf16[4,128,320]{2,1,0:T(8,128)(2,1)S(1)}, u32[]{:S(2)}) copy-start(bf16[4,128,320]{2,1,0:T(8,128)(2,1)S(1)} %slice_bitcast_fusion.19) | copy-start | bytes 983044 | tf_op jit(solution)/shard_map/while
  477.9 19.4 %collective-permute-start.2 = (bf16[1,40960]{1,0:T(2,128)(2,1)S(1)}, bf16[1,40960]{1,0:T(2,128)(2,1)S(1)}, u32[]{:S(2)}, u32[]{:S(2)}) collective-permute-start(bf16[1,40960]{1,0:T(2,128)(2,1)S(1)} %get-tuple-element.955), channel_id=1, source_target_pairs={{0,1},{1,2},{2,3},{3,4},{4,5},{5,6},{6,7},{8,9},{9,10},{10,11},{11... | collective-permute-start | bytes 245768 | tf_op jit(solution)/shard_map/while/body/eval_jaxpr/ppermute | solution.py:23
  482.1 15.2 %collective-permute-start.3 = (bf16[1,40960]{1,0:T(2,128)(2,1)S(1)}, bf16[1,40960]{1,0:T(2,128)(2,1)S(1)}, u32[]{:S(2)}, u32[]{:S(2)}) collective-permute-start(bf16[1,40960]{1,0:T(2,128)(2,1)S(1)} %get-tuple-element.956), channel_id=1, source_target_pairs={{1,0},{2,1},{3,2},{4,3},{5,4},{6,5},{7,6},{9,8},{10,9},{11,10},{12... | collective-permute-start | bytes 245768 | tf_op jit(solution)/shard_map/while/body/eval_jaxpr/ppermute | solution.py:24
  502.4 3.1 copy-start.16
  526.6 2.6 collective-permute-start.4
  527.9 4.2 collective-permute-start.5
  555.5 3.1 copy-start.18
  571.3 8.9 copy-start.8
  571.6 4.6 collective-permute-start.6
  573.2 4.0 collective-permute-start.7
  578.9 20.0 %collective-permute-start.9 = (bf16[6,128,320]{1,2,0:T(8,128)(2,1)}, bf16[6,128,320]{1,2,0:T(8,128)(2,1)S(1)}, u32[]{:S(2)}, u32[]{:S(2)}) collective-permute-start(bf16[6,128,320]{1,2,0:T(8,128)(2,1)} %pad_maximum_fusion.7), channel_id=1, source_target_pairs={{0,24},{1,25},{2,26},{3,27},{4,28},{5,29},{6,30},{7,31}} | collective-permute-start | bytes 1474568 | tf_op jit(solution)/shard_map/while/body/eval_jaxpr/ppermute | solution.py:32
  586.6 7.2 copy-start.24
  597.6 4.3 collective-permute-start.8
  604.6 5.8 collective-permute-start
  608.8 5.3 collective-permute-start.1
  610.4 14.7 %copy-start = (bf16[4,128,320]{2,1,0:T(8,128)(2,1)}, bf16[4,128,320]{2,1,0:T(8,128)(2,1)S(1)}, u32[]{:S(2)}) copy-start(bf16[4,128,320]{2,1,0:T(8,128)(2,1)S(1)} %slice_bitcast_fusion.19) | copy-start | bytes 983044 | tf_op jit(solution)/shard_map/while
  617.2 22.8 %collective-permute-start.2 = (bf16[1,40960]{1,0:T(2,128)(2,1)S(1)}, bf16[1,40960]{1,0:T(2,128)(2,1)S(1)}, u32[]{:S(2)}, u32[]{:S(2)}) collective-permute-start(bf16[1,40960]{1,0:T(2,128)(2,1)S(1)} %get-tuple-element.955), channel_id=1, source_target_pairs={{0,1},{1,2},{2,3},{3,4},{4,5},{5,6},{6,7},{8,9},{9,10},{10,11},{11... | collective-permute-start | bytes 245768 | tf_op jit(solution)/shard_map/while/body/eval_jaxpr/ppermute | solution.py:23
  623.8 16.2 %collective-permute-start.3 = (bf16[1,40960]{1,0:T(2,128)(2,1)S(1)}, bf16[1,40960]{1,0:T(2,128)(2,1)S(1)}, u32[]{:S(2)}, u32[]{:S(2)}) collective-permute-start(bf16[1,40960]{1,0:T(2,128)(2,1)S(1)} %get-tuple-element.956), channel_id=1, source_target_pairs={{1,0},{2,1},{3,2},{4,3},{5,4},{6,5},{7,6},{9,8},{10,9},{11,10},{12... | collective-permute-start | bytes 245768 | tf_op jit(solution)/shard_map/while/body/eval_jaxpr/ppermute | solution.py:24
  656.8 2.6 collective-permute-start.4
  658.1 4.9 collective-permute-start.5
  691.6 8.9 copy-start.8
  691.9 4.6 collective-permute-start.6
  693.5 4.0 collective-permute-start.7
  699.2 52.6 %collective-permute-start.9 = (bf16[6,128,320]{1,2,0:T(8,128)(2,1)}, bf16[6,128,320]{1,2,0:T(8,128)(2,1)S(1)}, u32[]{:S(2)}, u32[]{:S(2)}) collective-permute-start(bf16[6,128,320]{1,2,0:T(8,128)(2,1)} %pad_maximum_fusion.7), channel_id=1, source_target_pairs={{0,24},{1,25},{2,26},{3,27},{4,28},{5,29},{6,30},{7,31}} | collective-permute-start | bytes 1474568 | tf_op jit(solution)/shard_map/while/body/eval_jaxpr/ppermute | solution.py:32
  702.8 52.3 %collective-permute-start.8 = (bf16[2,64,640]{2,0,1:T(2,128)(2,1)S(1)}, bf16[2,64,640]{2,0,1:T(2,128)(2,1)S(1)}, u32[]{:S(2)}, u32[]{:S(2)}) collective-permute-start(bf16[2,64,640]{2,0,1:T(2,128)(2,1)S(1)} %get-tuple-element.1090), channel_id=1, source_target_pairs={{0,8},{8,16},{16,24},{1,9},{9,17},{17,25},{2,10},{10,18},{18,26},{... | collective-permute-start | bytes 491528 | tf_op jit(solution)/shard_map/while/body/eval_jaxpr/ppermute | solution.py:32
  755.6 5.0 collective-permute-start
  758.9 6.7 collective-permute-start.1
  760.6 16.7 %copy-start = (bf16[4,128,320]{2,1,0:T(8,128)(2,1)}, bf16[4,128,320]{2,1,0:T(8,128)(2,1)S(1)}, u32[]{:S(2)}) copy-start(bf16[4,128,320]{2,1,0:T(8,128)(2,1)S(1)} %slice_bitcast_fusion.19) | copy-start | bytes 983044 | tf_op jit(solution)/shard_map/while
  768.8 21.9 %collective-permute-start.2 = (bf16[1,40960]{1,0:T(2,128)(2,1)S(1)}, bf16[1,40960]{1,0:T(2,128)(2,1)S(1)}, u32[]{:S(2)}, u32[]{:S(2)}) collective-permute-start(bf16[1,40960]{1,0:T(2,128)(2,1)S(1)} %get-tuple-element.955), channel_id=1, source_target_pairs={{0,1},{1,2},{2,3},{3,4},{4,5},{5,6},{6,7},{8,9},{9,10},{10,11},{11... | collective-permute-start | bytes 245768 | tf_op jit(solution)/shard_map/while/body/eval_jaxpr/ppermute | solution.py:23
  775.9 14.8 %collective-permute-start.3 = (bf16[1,40960]{1,0:T(2,128)(2,1)S(1)}, bf16[1,40960]{1,0:T(2,128)(2,1)S(1)}, u32[]{:S(2)}, u32[]{:S(2)}) collective-permute-start(bf16[1,40960]{1,0:T(2,128)(2,1)S(1)} %get-tuple-element.956), channel_id=1, source_target_pairs={{1,0},{2,1},{3,2},{4,3},{5,4},{6,5},{7,6},{9,8},{10,9},{11,10},{12... | collective-permute-start | bytes 245768 | tf_op jit(solution)/shard_map/while/body/eval_jaxpr/ppermute | solution.py:24
  807.3 2.6 collective-permute-start.4
  808.7 4.9 collective-permute-start.5
  842.1 8.9 copy-start.8
  842.4 4.6 collective-permute-start.6
  844.0 4.0 collective-permute-start.7
  849.7 11.7 %collective-permute-start.9 = (bf16[6,128,320]{1,2,0:T(8,128)(2,1)}, bf16[6,128,320]{1,2,0:T(8,128)(2,1)S(1)}, u32[]{:S(2)}, u32[]{:S(2)}) collective-permute-start(bf16[6,128,320]{1,2,0:T(8,128)(2,1)} %pad_maximum_fusion.7), channel_id=1, source_target_pairs={{0,24},{1,25},{2,26},{3,27},{4,28},{5,29},{6,30},{7,31}} | collective-permute-start | bytes 1474568 | tf_op jit(solution)/shard_map/while/body/eval_jaxpr/ppermute | solution.py:32
  853.4 11.4 %collective-permute-start.8 = (bf16[2,64,640]{2,0,1:T(2,128)(2,1)S(1)}, bf16[2,64,640]{2,0,1:T(2,128)(2,1)S(1)}, u32[]{:S(2)}, u32[]{:S(2)}) collective-permute-start(bf16[2,64,640]{2,0,1:T(2,128)(2,1)S(1)} %get-tuple-element.1090), channel_id=1, source_target_pairs={{0,8},{8,16},{16,24},{1,9},{9,17},{17,25},{2,10},{10,18},{18,26},{... | collective-permute-start | bytes 491528 | tf_op jit(solution)/shard_map/while/body/eval_jaxpr/ppermute | solution.py:32
  865.4 5.3 collective-permute-start
  869.0 6.4 collective-permute-start.1
  870.7 14.7 %copy-start = (bf16[4,128,320]{2,1,0:T(8,128)(2,1)}, bf16[4,128,320]{2,1,0:T(8,128)(2,1)S(1)}, u32[]{:S(2)}) copy-start(bf16[4,128,320]{2,1,0:T(8,128)(2,1)S(1)} %slice_bitcast_fusion.19) | copy-start | bytes 983044 | tf_op jit(solution)/shard_map/while
  878.3 20.6 %collective-permute-start.2 = (bf16[1,40960]{1,0:T(2,128)(2,1)S(1)}, bf16[1,40960]{1,0:T(2,128)(2,1)S(1)}, u32[]{:S(2)}, u32[]{:S(2)}) collective-permute-start(bf16[1,40960]{1,0:T(2,128)(2,1)S(1)} %get-tuple-element.955), channel_id=1, source_target_pairs={{0,1},{1,2},{2,3},{3,4},{4,5},{5,6},{6,7},{8,9},{9,10},{10,11},{11... | collective-permute-start | bytes 245768 | tf_op jit(solution)/shard_map/while/body/eval_jaxpr/ppermute | solution.py:23
  884.1 14.9 %collective-permute-start.3 = (bf16[1,40960]{1,0:T(2,128)(2,1)S(1)}, bf16[1,40960]{1,0:T(2,128)(2,1)S(1)}, u32[]{:S(2)}, u32[]{:S(2)}) collective-permute-start(bf16[1,40960]{1,0:T(2,128)(2,1)S(1)} %get-tuple-element.956), channel_id=1, source_target_pairs={{1,0},{2,1},{3,2},{4,3},{5,4},{6,5},{7,6},{9,8},{10,9},{11,10},{12... | collective-permute-start | bytes 245768 | tf_op jit(solution)/shard_map/while/body/eval_jaxpr/ppermute | solution.py:24
  915.7 2.6 collective-permute-start.4
  917.0 4.8 collective-permute-start.5
  950.1 122.6 %copy-start.8 = (bf16[1,4,128,320]{2,3,1,0:T(8,128)(2,1)S(1)}, bf16[1,4,128,320]{2,3,1,0:T(8,128)(2,1)}, u32[]{:S(2)}) copy-start(bf16[1,4,128,320]{2,3,1,0:T(8,128)(2,1)} %get-tuple-element.1063) | copy-start | bytes 983044 | tf_op jit(solution)/shard_map/while
  950.4 4.6 collective-permute-start.6
  952.0 4.0 collective-permute-start.7
  957.6 125.7 %collective-permute-start.9 = (bf16[6,128,320]{1,2,0:T(8,128)(2,1)}, bf16[6,128,320]{1,2,0:T(8,128)(2,1)S(1)}, u32[]{:S(2)}, u32[]{:S(2)}) collective-permute-start(bf16[6,128,320]{1,2,0:T(8,128)(2,1)} %pad_maximum_fusion.7), channel_id=1, source_target_pairs={{0,24},{1,25},{2,26},{3,27},{4,28},{5,29},{6,30},{7,31}} | collective-permute-start | bytes 1474568 | tf_op jit(solution)/shard_map/while/body/eval_jaxpr/ppermute | solution.py:32
  1075.3 11.4 %collective-permute-start.8 = (bf16[2,64,640]{2,0,1:T(2,128)(2,1)S(1)}, bf16[2,64,640]{2,0,1:T(2,128)(2,1)S(1)}, u32[]{:S(2)}, u32[]{:S(2)}) collective-permute-start(bf16[2,64,640]{2,0,1:T(2,128)(2,1)S(1)} %get-tuple-element.1090), channel_id=1, source_target_pairs={{0,8},{8,16},{16,24},{1,9},{9,17},{17,25},{2,10},{10,18},{18,26},{... | collective-permute-start | bytes 491528 | tf_op jit(solution)/shard_map/while/body/eval_jaxpr/ppermute | solution.py:32
  (5 other events, 3.9 us)
Sparse Core Ops, SparseCore 0:
  1089.9 25.9 reduce-scatter.1
